TPU v7x, 512 devices: a whole 4x8x8 slice. The times are simulated.
512 devices in a mesh: src: 16 (over z, core), row: 32 (over x, y).
Axes of the slice: x: 4, y: 8, z: 8, core: 2. Of those that a mesh axis runs over, the one named last changes fastest.
Arguments:
- spec_re: bfloat16 [1024, 1024], P('row'), may hold values from -18 to 18
- spec_im: bfloat16 [1024, 1024], P('row'), may hold values from -18 to 18
- target: float32 [1024, 1024], P('row'), may hold values from 0.3 to 1.5
- weights: float32 [128], P('src'), may hold values from 0.25 to 2.5
- cent_row: int32 [128], P('src'), may hold values from 128 to 895
- cent_col: int32 [128], P('src'), may hold values from 128 to 895
Outputs:
- grad_re: float32 [1024, 1024], P('row')
- grad_im: float32 [1024, 1024], P('row')
Inputs may be any that keep to these rules, and one draw needn't show every extreme that they name: Every pupil disk of radius 128 about (cent_row, cent_col) lies inside the band.
All inputs are finite; a program needn't handle non-finite values.
Results may differ from a plain program's by a relative error of at most 0.0072.
Values may be sent and summed in bfloat16 or wider, within the bound.
No kernel may reach another device: no remote copies, remote signals or barrier semaphores. Data moves between devices by JAX's collectives and lax.ppermute only.
A program may use at most 128 MiB of HBM per device.

v0:
```python
import math
import jax
import jax.numpy as jnp
from jax import lax
from jax.sharding import PartitionSpec as P

RAD = 128
WIN = 384


def make_tables(band):
    position = jnp.arange(band, dtype=jnp.int32)
    phase = position[:, None] * position[None, :] % band
    angle = phase.astype(jnp.float32) * (2.0 * math.pi / band)
    factor = 1.0 / math.sqrt(band)
    return (
        (jnp.cos(angle) * factor).astype(jnp.bfloat16),
        (jnp.sin(angle) * factor).astype(jnp.bfloat16),
    )


def local(spec_re, spec_im, target, weights, cent_row, cent_col):
    rows_dev, band = spec_re.shape
    cols_dev = target.shape[0]
    points_dev = weights.shape[0]
    total_points = points_dev * lax.axis_size("src")
    cosine, sine = make_tables(band)
    tables_joined = jnp.concatenate([cosine, sine], axis=1)
    row_first = lax.axis_index("row") * rows_dev
    window_index = jnp.arange(WIN, dtype=jnp.int32)
    zero_value = jnp.zeros((), jnp.bfloat16)
    stacked = jnp.stack([spec_re, spec_im], axis=0)

    def window_starts(centre_cols):
        return jnp.clip(centre_cols - RAD, 0, band - WIN)

    def disk_window(first_row, row_count, centre_rows, centre_cols, starts):
        rows_here = first_row + jnp.arange(row_count, dtype=jnp.int32)
        row_gap = rows_here[None, :] - centre_rows[:, None]
        col_gap = starts[:, None] + window_index[None, :] - centre_cols[:, None]
        return row_gap[:, :, None] ** 2 + col_gap[:, None, :] ** 2 <= RAD * RAD

    col_first = lax.axis_index("row") * cols_dev
    narrow = jnp.concatenate(
        [
            lax.dynamic_slice_in_dim(cosine, col_first, cols_dev, 1),
            lax.dynamic_slice_in_dim(sine, col_first, cols_dev, 1),
        ],
        axis=1,
    )
    starts_all = window_starts(cent_col)
    narrow_windows = jax.vmap(lambda start: lax.dynamic_slice_in_dim(narrow, start, WIN, 0))(
        starts_all
    )
    spectrum_piece = lax.all_gather(stacked, "row", axis=1, tiled=True)
    inside_disk = disk_window(jnp.int32(0), spectrum_piece.shape[1], cent_row, cent_col, starts_all)
    pieces = jax.vmap(lambda start: lax.dynamic_slice_in_dim(spectrum_piece, start, WIN, 2))(
        starts_all
    )
    masked = jnp.where(inside_disk[:, None], pieces, zero_value)
    product = jnp.einsum(
        "pckl,plz->pckz", masked, narrow_windows, preferred_element_type=jnp.float32
    )
    real_part = product[:, 0, :, :cols_dev] - product[:, 1, :, cols_dev:]
    imag_part = product[:, 0, :, cols_dev:] + product[:, 1, :, :cols_dev]
    received = jnp.stack([real_part, imag_part], axis=1).astype(jnp.bfloat16)
    product = jnp.einsum(
        "pcky,kz->pcyz", received, tables_joined, preferred_element_type=jnp.float32
    )
    field_re = product[:, 0, :, :band] - product[:, 1, :, band:]
    field_im = product[:, 0, :, band:] + product[:, 1, :, :band]
    field = jnp.stack([field_re, field_im], axis=1)
    power = field[:, 0] * field[:, 0] + field[:, 1] * field[:, 1]
    local_power = jnp.sum(weights[:, None, None] * power, axis=0) / total_points
    intensity = lax.psum(local_power, "src")
    mismatch = intensity - target
    grad_field = (2.0 * weights[:, None, None, None] * mismatch[None, None] * field).astype(
        jnp.bfloat16
    )
    product = jnp.einsum(
        "pcyx,xz->pcyz", grad_field, tables_joined, preferred_element_type=jnp.float32
    )
    adj_re = product[:, 0, :, :band] + product[:, 1, :, band:]
    adj_im = product[:, 1, :, :band] - product[:, 0, :, band:]
    adjoint = jnp.stack([adj_re, adj_im], axis=1).astype(jnp.bfloat16)
    returned = lax.all_to_all(adjoint, "row", split_axis=3, concat_axis=2, tiled=True)
    starts = window_starts(cent_col)
    inside_disk = disk_window(row_first, rows_dev, cent_row, cent_col, starts)
    col_tables = jax.vmap(
        lambda start: jnp.concatenate(
            [
                lax.dynamic_slice_in_dim(cosine, start, WIN, 1),
                lax.dynamic_slice_in_dim(sine, start, WIN, 1),
            ],
            axis=1,
        )
    )(starts)
    result = jnp.einsum("pcyk,pyz->pckz", returned, col_tables, preferred_element_type=jnp.float32)
    term_re = result[:, 0, :, :WIN] + result[:, 1, :, WIN:]
    term_im = result[:, 1, :, :WIN] - result[:, 0, :, WIN:]
    zero_float = jnp.zeros((), jnp.float32)
    terms_re = jnp.where(inside_disk, term_re, zero_float)
    terms_im = jnp.where(inside_disk, term_im, zero_float)
    starts_local = window_starts(cent_col)
    local_re = jnp.zeros((rows_dev, band), jnp.float32)
    local_im = jnp.zeros((rows_dev, band), jnp.float32)
    for point in range(points_dev):
        start = starts_local[point]
        old_re = lax.dynamic_slice_in_dim(local_re, start, WIN, 1)
        old_im = lax.dynamic_slice_in_dim(local_im, start, WIN, 1)
        local_re = lax.dynamic_update_slice_in_dim(local_re, old_re + terms_re[point], start, 1)
        local_im = lax.dynamic_update_slice_in_dim(local_im, old_im + terms_im[point], start, 1)
    grad_re, grad_im = lax.psum((local_re, local_im), "src")
    return (grad_re, grad_im)


def solution(mesh):
    return jax.shard_map(
        local,
        mesh=mesh,
        in_specs=(P("row", None), P("row", None), P("row", None), P("src"), P("src"), P("src")),
        out_specs=(P("row", None), P("row", None)),
        check_vma=False,
    )
```

profile of v0, /device:TPU:1, one launch (start us, length us, event | category | flops | bytes accessed | tf_op | source)
XLA Modules:
  0.0 504.2 jit_solution(15990547782452756728)
XLA Ops:
  9.6 15.8 %multiply_convert_fusion = bf16[1024,1024]{1,0:T(8,128)(2,1)S(1)} fusion(), kind=kLoop, calls=%fused_computation.23 | loop fusion | flops 16777216 | bytes 2097152 | tf_op jit(solution)/shard_map/convert_element_type | solution.py:18
  25.4 15.7 %multiply_convert_fusion.1 = bf16[1024,1024]{1,0:T(8,128)(2,1)S(1)} fusion(), kind=kLoop, calls=%fused_computation.24 | loop fusion | flops 16777216 | bytes 2097152 | tf_op jit(solution)/shard_map/convert_element_type | solution.py:17
  41.8 3.6 add_compare_fusion
  45.4 9.7 %while.9 = (s32[]{:T(128)}, bf16[1024,64]{1,0:T(8,128)(2,1)S(1)}, s32[8,2]{0,1:T(2,128)S(1)}, bf16[8,384,64]{2,1,0:T(8,128)(2,1)S(1)}) while((s32[]{:T(128)}, bf16[1024,64]{1,0:T(8,128)(2,1)S(1)}, s32[8,2]{0,1:T(2,128)S(1)}, bf16[8,384,64]{2,1,0:T(8,128)(2,1)S(1)}) %tuple.83), condition=%wide.while_cond.1.clone, body=%wide.while_body.1.sunk.clone | while | flops 2 | bytes 196705 | solution.py:52
  55.0 3.1 broadcast.133.clone
  58.2 30.4 %while.11 = (s32[]{:T(128)}, bf16[1024,1024]{1,0:T(8,128)(2,1)}, s32[8,2]{0,1:T(2,128)S(1)}, bf16[8,1024,384]{2,1,0:T(8,128)(2,1)}) while((s32[]{:T(128)}, bf16[1024,1024]{1,0:T(8,128)(2,1)}, s32[8,2]{0,1:T(2,128)S(1)}, bf16[8,1024,384]{2,1,0:T(8,128)(2,1)}) %tuple.100), condition=%wide.while_cond.3.clone, body=%wide.while_body.3.sunk.clone | while | flops 2 | bytes 1573469 | solution.py:93
  58.8 3.2 bitcast_dynamic-update-slice_fusion.15
  62.6 3.1 bitcast_dynamic-update-slice_fusion.15
  66.4 3.1 bitcast_dynamic-update-slice_fusion.15
  70.2 3.2 bitcast_dynamic-update-slice_fusion.15
  74.1 3.1 bitcast_dynamic-update-slice_fusion.15
  77.9 3.1 bitcast_dynamic-update-slice_fusion.15
  81.6 3.1 bitcast_dynamic-update-slice_fusion.15
  85.4 3.2 bitcast_dynamic-update-slice_fusion.15
  88.5 12.4 %all-gather.2.cloned.1.call-done = bf16[2,1024,1024]{2,1,0:T(8,128)(2,1)} async-done(((bf16[2,32,1024]{2,1,0:T(8,128)(2,1)}), bf16[2,1024,1024]{2,1,0:T(8,128)(2,1)}) %all-gather.2.cloned.1.call-update) | async-done | bytes 4194320 | tf_op jit(solution)/shard_map/all_gather | solution.py:55
  101.0 37.9 %while.8 = (s32[]{:T(128)}, bf16[2,1024,1024]{2,1,0:T(8,128)(2,1)}, s32[8,3]{0,1:T(4,128)S(1)}, bf16[8,2,1024,384]{3,2,1,0:T(8,128)(2,1)}) while((s32[]{:T(128)}, bf16[2,1024,1024]{2,1,0:T(8,128)(2,1)}, s32[8,3]{0,1:T(4,128)S(1)}, bf16[8,2,1024,384]{3,2,1,0:T(8,128)(2,1)}) %tuple.80), condition=%wide.while_cond.clone, body=%wide.while_body.sunk.clone | while | flops 2 | bytes 3146341 | solution.py:57
  101.5 4.2 bitcast_dynamic-update-slice_fusion.12
  106.3 4.2 bitcast_dynamic-update-slice_fusion.12
  111.0 4.2 bitcast_dynamic-update-slice_fusion.12
  115.8 4.2 bitcast_dynamic-update-slice_fusion.12
  120.6 4.1 bitcast_dynamic-update-slice_fusion.12
  125.3 4.1 bitcast_dynamic-update-slice_fusion.12
  129.9 4.2 bitcast_dynamic-update-slice_fusion.12
  134.7 4.2 bitcast_dynamic-update-slice_fusion.12
  138.9 7.7 %fusion = f32[8,2,1024,64]{2,3,1,0:T(8,128)S(1)} fusion(bf16[8,2,1024,384]{3,2,1,0:T(8,128)(2,1)} %get-tuple-element.9, pred[8,1024,384]{2,1,0:T(8,128)(4,1)} %add_compare_fusion, bf16[8,384,64]{2,1,0:T(8,128)(2,1)S(1)} %get-tuple-element.17), kind=kOutput, calls=%fused_computation.9 | convolution fusion | flops 811597824 | bytes 20316160 | tf_op jit(solution)/shard_map/pckl,plz->pckz/dot_general | solution.py:61
  148.2 2.3 fusion.12
  150.5 1.6 fusion.22
  152.9 116.9 %all-reduce.7.cloned.1.call-done = f32[32,1024]{1,0:T(8,128)} async-done(((f32[32,1024]{1,0:T(8,128)}), f32[32,1024]{1,0:T(8,128)}) %all-reduce.7.cloned.1.call-update) | async-done | bytes 131088 | tf_op jit(solution)/shard_map/psum | solution.py:75
  270.9 4.3 fusion.11
  275.6 7.5 %copy.13 = bf16[8,2,32,1024]{2,1,0,3:T(2,128)(2,1)} copy(bf16[8,2,32,1024]{3,2,1,0:T(8,128)(2,1)S(1)} %pad_maximum_fusion) | data formatting | bytes 2097152 | tf_op jit(solution)/shard_map/stack | solution.py:85
  283.2 9.9 %reshape.192 = bf16[32,2,8192]{2,1,0:T(2,128)(2,1)} reshape(bf16[1024,8,2,32]{3,2,1,0:T(2,128)(2,1)} %bitcast.159) | data formatting | bytes 2097152
  293.1 9.3 %all-to-all-start = ((bf16[32,2,8192]{2,1,0:T(2,128)(2,1)}), bf16[32,2,8192]{2,1,0:T(2,128)(2,1)S(1)}, u32[]{:S(2)}, u32[]{:S(2)}) async-start(bf16[32,2,8192]{2,1,0:T(2,128)(2,1)} %reshape.192), calls=%async_computation | async-start | bytes 2097152 | tf_op jit(solution)/shard_map/all_to_all | solution.py:86
  318.1 3.2 broadcast.133.clone.1
  321.4 19.9 %while.10 = (s32[]{:T(128)}, bf16[1024,1024]{1,0:T(8,128)(2,1)S(1)}, s32[8,2]{0,1:T(2,128)S(1)}, bf16[8,1024,384]{2,1,0:T(8,128)(2,1)}) while((s32[]{:T(128)}, bf16[1024,1024]{1,0:T(8,128)(2,1)S(1)}, s32[8,2]{0,1:T(2,128)S(1)}, bf16[8,1024,384]{2,1,0:T(8,128)(2,1)}) %tuple.101), condition=%wide.while_cond.2.clone, body=%wide.while_body.2.sunk.clone | while | flops 2 | bytes 1573469 | solution.py:92
  321.9 1.9 bitcast_dynamic-update-slice_fusion.14
  324.4 1.9 bitcast_dynamic-update-slice_fusion.14
  326.9 1.9 bitcast_dynamic-update-slice_fusion.14
  329.4 1.9 bitcast_dynamic-update-slice_fusion.14
  331.9 1.9 bitcast_dynamic-update-slice_fusion.14
  334.4 1.9 bitcast_dynamic-update-slice_fusion.14
  336.9 1.9 bitcast_dynamic-update-slice_fusion.14
  339.4 1.9 bitcast_dynamic-update-slice_fusion.14
  341.3 3.6 reshape.193
  344.8 6.9 %copy.25 = bf16[8,2,32,32,32]{2,3,4,1,0:T(8,128)(2,1)} copy(bf16[8,2,32,32,32]{2,1,0,4,3:T(2,128)(2,1)} %bitcast.160) | data formatting | bytes 2097152 | tf_op jit(solution)/shard_map/all_to_all | solution.py:86
  351.8 6.2 %all_to_all.16 = bf16[8,2,1024,32]{2,3,1,0:T(8,128)(2,1)S(1)} reshape(bf16[8,2,32,32,32]{3,2,4,1,0:T(8,128)(2,1)} %bitcast.161) | data formatting | bytes 2097152 | tf_op jit(solution)/shard_map/all_to_all | solution.py:86
  357.9 5.8 %fusion.2 = f32[8,2,32,768]{3,2,1,0:T(8,128)S(1)} fusion(bf16[8,2,1024,32]{2,3,1,0:T(8,128)(2,1)S(1)} %all_to_all.16, bf16[8,1024,384]{2,1,0:T(8,128)(2,1)} %get-tuple-element.33, bf16[8,1024,384]{2,1,0:T(8,128)(2,1)} %get-tuple-element.25), kind=kOutput, calls=%fused_computation.12 | convolution fusion | flops 830472192 | bytes 15204352 | tf_op jit(solution)/shard_map/pcyk,pyz->pckz/dot_general | solution.py:98
  376.7 117.8 %all-reduce.9.cloned.1.call-done = (f32[32,1024]{1,0:T(8,128)}, f32[32,1024]{1,0:T(8,128)}) async-done(((f32[32,1024]{1,0:T(8,128)}, f32[32,1024]{1,0:T(8,128)}), (f32[32,1024]{1,0:T(8,128)}, f32[32,1024]{1,0:T(8,128)})) %all-reduce.9.cloned.1.call-update) | async-done | bytes 262160 | tf_op jit(solution)/shard_map/psum | solution.py:113
  494.6 1.6 copy.73
  (151 shorter events, 45.8 us)
Async XLA Ops:
  7.2 34.5 %copy-start.7 = (s32[8]{0:T(128)S(1)}, s32[8]{0:T(128)}, u32[]{:S(2)}) copy-start(s32[8]{0:T(128)} %param.11) | copy-start | bytes 100
  7.2 34.4 %copy-start.5 = (s32[8]{0:T(128)S(1)}, s32[8]{0:T(128)}, u32[]{:S(2)}) copy-start(s32[8]{0:T(128)} %param.10) | copy-start | bytes 100
  7.2 93.8 %all-gather.2.cloned.1.call-start = ((), (), s32[]{:S(2)}) async-start(), calls=%async_computation.1 | async-start | bytes 4325376 | tf_op jit(solution)/shard_map/all_gather | solution.py:55
  8.8 261.0 %all-reduce.7.cloned.1.call-start = ((), (), s32[]{:S(2)}) async-start(), calls=%async_computation.2 | async-start | bytes 262144 | tf_op jit(solution)/shard_map/psum | solution.py:75
  25.4 15.7 %copy-start = (bf16[1024,1024]{1,0:T(8,128)(2,1)}, bf16[1024,1024]{1,0:T(8,128)(2,1)S(1)}, u32[]{:S(2)}) copy-start(bf16[1024,1024]{1,0:T(8,128)(2,1)S(1)} %multiply_convert_fusion) | copy-start | bytes 6291460
  146.6 1.6 copy-start.1
  148.2 2.4 copy-start.6
  150.5 119.3 %copy-start.4 = (f32[32,1024]{1,0:T(8,128)S(1)}, f32[32,1024]{1,0:T(8,128)}, u32[]{:S(2)}) copy-start(f32[32,1024]{1,0:T(8,128)} %param.8) | copy-start | bytes 393220
  293.1 48.2 %all-to-all-start = ((bf16[32,2,8192]{2,1,0:T(2,128)(2,1)}), bf16[32,2,8192]{2,1,0:T(2,128)(2,1)S(1)}, u32[]{:S(2)}, u32[]{:S(2)}) async-start(bf16[32,2,8192]{2,1,0:T(2,128)(2,1)} %reshape.192), calls=%async_computation | async-start | bytes 2097152 | tf_op jit(solution)/shard_map/all_to_all | solution.py:86
  302.4 192.2 %all-reduce.9.cloned.1.call-start = ((), (), s32[]{:S(2)}) async-start(), calls=%async_computation.3 | async-start | bytes 524288 | tf_op jit(solution)/shard_map/psum | solution.py:113
  370.0 6.1 %copy-start.3 = (f32[32,1024]{1,0:T(8,128)}, f32[32,1024]{1,0:T(8,128)S(1)}, u32[]{:S(2)}) copy-start(f32[32,1024]{1,0:T(8,128)S(1)} %dynamic_update_slice.55) | copy-start | bytes 393220
  376.0 0.7 copy-start.2
Sparse Core Ops, SparseCore 0:
  11.7 89.1 all-gather.1
  153.0 116.7 all-reduce.6
  376.8 117.6 all-reduce.8
where the time goes:
time: 506 us; the launch traced here: 504 us
  waiting for transfers between devices  247 us (49%)
  local copies, waits for them, and re-layouts  155 us (31%)
  other arithmetic  43.3 us (9%)
  between operations  29.3 us (6%)
  matrix products  20.2 us (4%)
  starting transfers between devices  9.38 us (2%)
    psum x1, waiting for transfers between devices, local(): grad_re, grad_im = lax.psum((local_re, local_im), 'src')  118 us
    psum x1, waiting for transfers between devices, local(): intensity = lax.psum(local_power, 'src')  117 us
    gather x96, local copies, waits for them, and re-layouts  97.7 us
    unnamed x22, local copies, waits for them, and re-layouts  24.9 us
    convert_element_type x1, other arithmetic, make_tables(): (jnp.sin(angle) * factor).astype(jnp.bfloat16)  15.8 us
    convert_element_type x1, other arithmetic, make_tables(): (jnp.cos(angle) * factor).astype(jnp.bfloat16)  15.7 us
    all_to_all x2, local copies, waits for them, and re-layouts, local(): lax.all_to_all(adjoint, 'row', split_axis=3, concat_axis=2, tiled=True)  13.1 us
    all_gather x1, waiting for transfers between devices, local(): spectrum_piece = lax.all_gather(stacked, 'row', axis=1, tiled=True)  12.4 us
  transfers between devices with their start and end apart: 4, of which 3 were waited for; matrix products, arithmetic and copies ran while one was open for 20% of the time, Pallas kernels for 0%

commit v1 on v0

--- a/solution.py
+++ b/solution.py
@@ -72,7 +72,8 @@
     field = jnp.stack([field_re, field_im], axis=1)
     power = field[:, 0] * field[:, 0] + field[:, 1] * field[:, 1]
     local_power = jnp.sum(weights[:, None, None] * power, axis=0) / total_points
-    intensity = lax.psum(local_power, "src")
+    parts = lax.all_gather(local_power, "src")
+    intensity = jnp.sum(parts, axis=0)
     mismatch = intensity - target
     grad_field = (2.0 * weights[:, None, None, None] * mismatch[None, None] * field).astype(
         jnp.bfloat16

time: 506 us -> 432 us (0.85)
  waiting for transfers between devices: 247 us -> 167 us
    psum x1 -> x0, waiting for transfers between devices: 117 us -> none  [local(): intensity = lax.psum(local_power, 'src')]
    all_gather x1, waiting for transfers between devices: 12.4 us -> 40.1 us  [local(): spectrum_piece = lax.all_gather(stacked, 'row', axis=1, tiled=True)]
    all_gather x0 -> x1, waiting for transfers between devices: none -> 11.6 us  [local(): parts = lax.all_gather(local_power, 'src')]
  transfers between devices with their start and end apart: 4 -> 4, of which waited for: 3 -> 3; matrix products, arithmetic and copies ran while one was open for 20% -> 25% of each run, Pallas kernels for 0% -> 0%
where the time goes in v1:
time: 432 us; the launch traced here: 431 us
  waiting for transfers between devices  167 us (39%)
  local copies, waits for them, and re-layouts  160 us (37%)
  other arithmetic  44.1 us (10%)
  between operations  29.8 us (7%)
  matrix products  20.4 us (5%)
  starting transfers between devices  9.38 us (2%)
    psum x1, waiting for transfers between devices, local(): grad_re, grad_im = lax.psum((local_re, local_im), 'src')  116 us
    gather x96, local copies, waits for them, and re-layouts  103 us
    all_gather x1, waiting for transfers between devices, local(): spectrum_piece = lax.all_gather(stacked, 'row', axis=1, tiled=True)  40.1 us
    unnamed x22, local copies, waits for them, and re-layouts  24.9 us
    convert_element_type x1, other arithmetic, make_tables(): (jnp.sin(angle) * factor).astype(jnp.bfloat16)  15.8 us
    convert_element_type x1, other arithmetic, make_tables(): (jnp.cos(angle) * factor).astype(jnp.bfloat16)  15.7 us
    all_to_all x2, local copies, waits for them, and re-layouts, local(): lax.all_to_all(adjoint, 'row', split_axis=3, concat_axis=2, tiled=True)  13 us
    all_gather x1, waiting for transfers between devices, local(): parts = lax.all_gather(local_power, 'src')  11.6 us
  transfers between devices with their start and end apart: 4, of which 3 were waited for; matrix products, arithmetic and copies ran while one was open for 25% of the time, Pallas kernels for 0%

profile of v1, /device:TPU:1, one launch (start us, length us, event | category | flops | bytes accessed | tf_op | source)
XLA Modules:
  0.0 430.7 jit_solution(12978605900237988577)
XLA Ops:
  9.6 15.8 %multiply_convert_fusion = bf16[1024,1024]{1,0:T(8,128)(2,1)S(1)} fusion(), kind=kLoop, calls=%fused_computation.23 | loop fusion | flops 16777216 | bytes 2097152 | tf_op jit(solution)/shard_map/convert_element_type | solution.py:18
  25.4 15.7 %multiply_convert_fusion.1 = bf16[1024,1024]{1,0:T(8,128)(2,1)S(1)} fusion(), kind=kLoop, calls=%fused_computation.24 | loop fusion | flops 16777216 | bytes 2097152 | tf_op jit(solution)/shard_map/convert_element_type | solution.py:17
  41.7 3.6 add_compare_fusion
  45.3 15.5 %while.9 = (s32[]{:T(128)}, bf16[1024,64]{1,0:T(8,128)(2,1)S(1)}, s32[8,2]{0,1:T(2,128)S(1)}, bf16[8,384,64]{2,1,0:T(8,128)(2,1)}) while((s32[]{:T(128)}, bf16[1024,64]{1,0:T(8,128)(2,1)S(1)}, s32[8,2]{0,1:T(2,128)S(1)}, bf16[8,384,64]{2,1,0:T(8,128)(2,1)}) %tuple.83), condition=%wide.while_cond.1.clone, body=%wide.while_body.1.sunk.clone | while | flops 2 | bytes 148061 | solution.py:52
  60.8 40.1 %all-gather.4.cloned.1.call-done = bf16[2,1024,1024]{2,1,0:T(8,128)(2,1)} async-done(((bf16[2,32,1024]{2,1,0:T(8,128)(2,1)}), bf16[2,1024,1024]{2,1,0:T(8,128)(2,1)}) %all-gather.4.cloned.1.call-update) | async-done | bytes 4194320 | tf_op jit(solution)/shard_map/all_gather | solution.py:55
  100.9 37.9 %while.8 = (s32[]{:T(128)}, bf16[2,1024,1024]{2,1,0:T(8,128)(2,1)}, s32[8,3]{0,1:T(4,128)S(1)}, bf16[8,2,1024,384]{3,2,1,0:T(8,128)(2,1)}) while((s32[]{:T(128)}, bf16[2,1024,1024]{2,1,0:T(8,128)(2,1)}, s32[8,3]{0,1:T(4,128)S(1)}, bf16[8,2,1024,384]{3,2,1,0:T(8,128)(2,1)}) %tuple.80), condition=%wide.while_cond.clone, body=%wide.while_body.sunk.clone | while | flops 2 | bytes 3146341 | solution.py:57
  101.5 4.2 bitcast_dynamic-update-slice_fusion.12
  106.3 4.2 bitcast_dynamic-update-slice_fusion.12
  111.0 4.2 bitcast_dynamic-update-slice_fusion.12
  115.8 4.2 bitcast_dynamic-update-slice_fusion.12
  120.5 4.1 bitcast_dynamic-update-slice_fusion.12
  125.3 4.1 bitcast_dynamic-update-slice_fusion.12
  129.9 4.2 bitcast_dynamic-update-slice_fusion.12
  134.7 4.2 bitcast_dynamic-update-slice_fusion.12
  138.9 7.9 %fusion = f32[8,2,1024,64]{2,3,1,0:T(8,128)S(1)} fusion(bf16[8,2,1024,384]{3,2,1,0:T(8,128)(2,1)} %get-tuple-element.9, pred[8,1024,384]{2,1,0:T(8,128)(4,1)} %add_compare_fusion, bf16[8,384,64]{2,1,0:T(8,128)(2,1)} %get-tuple-element.17), kind=kOutput, calls=%fused_computation.9 | convolution fusion | flops 811597824 | bytes 20316160 | tf_op jit(solution)/shard_map/pckl,plz->pckz/dot_general | solution.py:61
  148.3 2.3 fusion.12
  150.7 1.6 fusion.22
  153.1 3.2 broadcast.142.clone
  156.3 29.4 %while.11 = (s32[]{:T(128)}, bf16[1024,1024]{1,0:T(8,128)(2,1)}, s32[8,2]{0,1:T(2,128)S(1)}, bf16[8,1024,384]{2,1,0:T(8,128)(2,1)}) while((s32[]{:T(128)}, bf16[1024,1024]{1,0:T(8,128)(2,1)}, s32[8,2]{0,1:T(2,128)S(1)}, bf16[8,1024,384]{2,1,0:T(8,128)(2,1)}) %tuple.100), condition=%wide.while_cond.3.clone, body=%wide.while_body.3.sunk.clone | while | flops 2 | bytes 1573469 | solution.py:94
  156.9 3.1 bitcast_dynamic-update-slice_fusion.15
  160.6 3.1 bitcast_dynamic-update-slice_fusion.15
  164.3 3.1 bitcast_dynamic-update-slice_fusion.15
  168.0 3.1 bitcast_dynamic-update-slice_fusion.15
  171.7 3.0 bitcast_dynamic-update-slice_fusion.15
  175.4 3.0 bitcast_dynamic-update-slice_fusion.15
  179.0 3.0 bitcast_dynamic-update-slice_fusion.15
  182.6 3.1 bitcast_dynamic-update-slice_fusion.15
  185.7 11.6 %all-gather.6.cloned.1.call-done = f32[512,1024]{1,0:T(8,128)} async-done(((f32[32,1024]{1,0:T(8,128)}), f32[512,1024]{1,0:T(8,128)}) %all-gather.6.cloned.1.call-update) | async-done | bytes 2097168 | tf_op jit(solution)/shard_map/all_gather | solution.py:75
  197.3 1.7 reduce_sum.19
  199.2 4.3 fusion.11
  204.0 7.5 %copy.18 = bf16[8,2,32,1024]{2,1,0,3:T(2,128)(2,1)} copy(bf16[8,2,32,1024]{3,2,1,0:T(8,128)(2,1)S(1)} %pad_maximum_fusion) | data formatting | bytes 2097152 | tf_op jit(solution)/shard_map/stack | solution.py:86
  211.5 9.9 %reshape.202 = bf16[32,2,8192]{2,1,0:T(2,128)(2,1)} reshape(bf16[1024,8,2,32]{3,2,1,0:T(2,128)(2,1)} %bitcast.160) | data formatting | bytes 2097152
  221.4 9.3 %all-to-all-start = ((bf16[32,2,8192]{2,1,0:T(2,128)(2,1)}), bf16[32,2,8192]{2,1,0:T(2,128)(2,1)S(1)}, u32[]{:S(2)}, u32[]{:S(2)}) async-start(bf16[32,2,8192]{2,1,0:T(2,128)(2,1)} %reshape.202), calls=%async_computation | async-start | bytes 2097152 | tf_op jit(solution)/shard_map/all_to_all | solution.py:87
  247.0 3.2 broadcast.142.clone.1
  250.2 19.9 %while.10 = (s32[]{:T(128)}, bf16[1024,1024]{1,0:T(8,128)(2,1)S(1)}, s32[8,2]{0,1:T(2,128)S(1)}, bf16[8,1024,384]{2,1,0:T(8,128)(2,1)}) while((s32[]{:T(128)}, bf16[1024,1024]{1,0:T(8,128)(2,1)S(1)}, s32[8,2]{0,1:T(2,128)S(1)}, bf16[8,1024,384]{2,1,0:T(8,128)(2,1)}) %tuple.101), condition=%wide.while_cond.2.clone, body=%wide.while_body.2.sunk.clone | while | flops 2 | bytes 1573469 | solution.py:93
  250.8 1.9 bitcast_dynamic-update-slice_fusion.14
  253.2 1.9 bitcast_dynamic-update-slice_fusion.14
  255.8 1.9 bitcast_dynamic-update-slice_fusion.14
  258.2 1.9 bitcast_dynamic-update-slice_fusion.14
  260.7 1.9 bitcast_dynamic-update-slice_fusion.14
  263.2 1.9 bitcast_dynamic-update-slice_fusion.14
  265.7 1.9 bitcast_dynamic-update-slice_fusion.14
  268.2 1.9 bitcast_dynamic-update-slice_fusion.14
  270.1 3.5 reshape.203
  273.6 6.8 %copy.30 = bf16[8,2,32,32,32]{2,3,4,1,0:T(8,128)(2,1)} copy(bf16[8,2,32,32,32]{2,1,0,4,3:T(2,128)(2,1)} %bitcast.161) | data formatting | bytes 2097152 | tf_op jit(solution)/shard_map/all_to_all | solution.py:87
  280.5 6.2 %all_to_all.16 = bf16[8,2,1024,32]{2,3,1,0:T(8,128)(2,1)S(1)} reshape(bf16[8,2,32,32,32]{3,2,4,1,0:T(8,128)(2,1)} %bitcast.162) | data formatting | bytes 2097152 | tf_op jit(solution)/shard_map/all_to_all | solution.py:87
  286.6 5.9 %fusion.2 = f32[8,2,32,768]{3,2,1,0:T(8,128)S(1)} fusion(bf16[8,2,1024,32]{2,3,1,0:T(8,128)(2,1)S(1)} %all_to_all.16, bf16[8,1024,384]{2,1,0:T(8,128)(2,1)} %get-tuple-element.33, bf16[8,1024,384]{2,1,0:T(8,128)(2,1)} %get-tuple-element.25), kind=kOutput, calls=%fused_computation.12 | convolution fusion | flops 830472192 | bytes 15204352 | tf_op jit(solution)/shard_map/pcyk,pyz->pckz/dot_general | solution.py:99
  305.4 115.6 %all-reduce.6.cloned.1.call-done = (f32[32,1024]{1,0:T(8,128)}, f32[32,1024]{1,0:T(8,128)}) async-done(((f32[32,1024]{1,0:T(8,128)}, f32[32,1024]{1,0:T(8,128)}), (f32[32,1024]{1,0:T(8,128)}, f32[32,1024]{1,0:T(8,128)})) %all-reduce.6.cloned.1.call-update) | async-done | bytes 262160 | tf_op jit(solution)/shard_map/psum | solution.py:114
  (152 shorter events, 52.2 us)
Async XLA Ops:
  7.2 34.4 %copy-start.7 = (s32[8]{0:T(128)S(1)}, s32[8]{0:T(128)}, u32[]{:S(2)}) copy-start(s32[8]{0:T(128)} %param.11) | copy-start | bytes 100
  7.2 34.5 %copy-start.5 = (s32[8]{0:T(128)S(1)}, s32[8]{0:T(128)}, u32[]{:S(2)}) copy-start(s32[8]{0:T(128)} %param.10) | copy-start | bytes 100
  7.2 93.8 %all-gather.4.cloned.1.call-start = ((), (), s32[]{:S(2)}) async-start(), calls=%async_computation.1 | async-start | bytes 4325376 | tf_op jit(solution)/shard_map/all_gather | solution.py:55
  8.8 188.5 %all-gather.6.cloned.1.call-start = ((), (), s32[]{:S(2)}) async-start(), calls=%async_computation.2 | async-start | bytes 2228224 | tf_op jit(solution)/shard_map/all_gather | solution.py:75
  25.4 15.7 %copy-start = (bf16[1024,1024]{1,0:T(8,128)(2,1)}, bf16[1024,1024]{1,0:T(8,128)(2,1)S(1)}, u32[]{:S(2)}) copy-start(bf16[1024,1024]{1,0:T(8,128)(2,1)S(1)} %multiply_convert_fusion) | copy-start | bytes 6291460
  146.7 1.6 copy-start.1
  148.3 2.4 copy-start.6
  156.3 42.8 %copy-start.4 = (f32[32,1024]{1,0:T(8,128)S(1)}, f32[32,1024]{1,0:T(8,128)}, u32[]{:S(2)}) copy-start(f32[32,1024]{1,0:T(8,128)} %param.8) | copy-start | bytes 393220
  221.4 48.6 %all-to-all-start = ((bf16[32,2,8192]{2,1,0:T(2,128)(2,1)}), bf16[32,2,8192]{2,1,0:T(2,128)(2,1)S(1)}, u32[]{:S(2)}, u32[]{:S(2)}) async-start(bf16[32,2,8192]{2,1,0:T(2,128)(2,1)} %reshape.202), calls=%async_computation | async-start | bytes 2097152 | tf_op jit(solution)/shard_map/all_to_all | solution.py:87
  230.7 190.3 %all-reduce.6.cloned.1.call-start = ((), (), s32[]{:S(2)}) async-start(), calls=%async_computation.3 | async-start | bytes 524288 | tf_op jit(solution)/shard_map/psum | solution.py:114
  298.7 6.1 %copy-start.3 = (f32[32,1024]{1,0:T(8,128)}, f32[32,1024]{1,0:T(8,128)S(1)}, u32[]{:S(2)}) copy-start(f32[32,1024]{1,0:T(8,128)S(1)} %dynamic_update_slice.55) | copy-start | bytes 393220
  304.7 0.7 copy-start.2
Sparse Core Ops, SparseCore 0:
  11.7 89.1 all-gather.3
  153.1 44.1 all-gather.5
  305.6 115.4 all-reduce.5
